TPU v7x, 128 devices: a whole 4x4x4 slice. The times are simulated.
128 devices in a mesh: cell: 32 (over x, z, y_hi), spec: 4 (over y_lo, core).
Axes of the slice: x: 4, y: 4 (y_hi: 2, y_lo: 2; y = y_hi * 2 + y_lo), z: 4, core: 2. Of those that a mesh axis runs over, the one named last changes fastest.
Arguments:
- fields: bfloat16 [4, 1024, 384], P('spec', 'cell'), may hold values from -6 to 6
- tensors: bfloat16 [16, 384, 384, 384], P('spec', 'cell'), may hold values from -0.0078125 to 0.0078125
- pair_table: int32 [4, 4], replicated, may hold values from 0 to 15, as said below
- plus_flux: float32 [4, 384, 384], P('spec'), may hold values from -0.3125 to 0.3125
- minus_flux: float32 [4, 384, 384], P('spec'), may hold values from -0.3125 to 0.3125
- face_limiter: int32 [4, 1024], P('spec', 'cell'), may hold values from 0 to 2
Outputs:
- new_field: float32 [4, 1024, 384], P('spec', 'cell')
- collision: float32 [4, 1024, 384], P('spec', 'cell')
Inputs may be any that keep to these rules, and one draw needn't show every extreme that they name: Row s of pair_table names each of the tensors s * 4 to s * 4 + 3 exactly once. `face_limiter`: 0 first order, 1 minmod slope, 2 monotonized central slope.
All inputs are finite; a program needn't handle non-finite values.
Results may differ from a plain program's by a relative error of at most 0.0004.
Values may be sent and summed in bfloat16 or wider, within the bound.
A program may use at most 64 MiB of HBM per device.

v0:
```python
import jax
import jax.numpy as jnp
from jax import lax
from jax.sharding import PartitionSpec as P


def with_halo(x, sides, width):
    for axis, dim in sides:
        size, length = (lax.axis_size(axis), x.shape[dim])
        up = [(i, (i + 1) % size) for i in range(size)]
        down = [(j, i) for i, j in up]
        last = lax.slice_in_dim(x, length - width, length, axis=dim)
        leading = lax.slice_in_dim(x, 0, width, axis=dim)
        before = lax.ppermute(last, axis, up)
        after = lax.ppermute(leading, axis, down)
        x = jnp.concatenate([before, x, after], axis=dim)
    return x


def shifted(x, axis, by):
    size = lax.axis_size(axis)
    return lax.ppermute(x, axis, [(i, (i + by) % size) for i in range(size)])


def minmod_two(first, second):
    return jnp.where(
        first * second > 0, jnp.sign(first) * jnp.minimum(jnp.abs(first), jnp.abs(second)), 0.0
    )


def minmod_three(first, second, third):
    same = (first * second > 0) & (second * third > 0)
    least = jnp.minimum(jnp.minimum(jnp.abs(first), jnp.abs(second)), jnp.abs(third))
    return jnp.where(same, jnp.sign(first) * least, 0.0)


def local(fields, tensors, pair_table, plus_flux, minus_flux, face_limiter):
    cells = fields.shape[1]
    species = lax.axis_size("spec")
    owner = lax.axis_index("spec")
    total_cells = cells * lax.axis_size("cell")
    out_modes = tensors.shape[1]
    table_row = lax.dynamic_index_in_dim(pair_table, owner, 0, keepdims=False)
    all_species = lax.all_gather(fields, "spec", axis=0, tiled=True)
    gathered = lax.all_gather(all_species, "cell", axis=1, tiled=True)
    own_rows = lax.dynamic_index_in_dim(gathered, owner, 0, keepdims=True)
    own_wide = own_rows[0].astype(jnp.float32)
    collision_part = jnp.zeros((total_cells, out_modes), jnp.float32)
    for partner in range(species):
        partner_rows = gathered[partner]
        local_pair = table_row[partner] - owner * species
        tensor = lax.dynamic_index_in_dim(tensors, local_pair, 0, keepdims=False)
        inner = jnp.einsum("cj,kij->cki", partner_rows, tensor, preferred_element_type=jnp.float32)
        collision_part = collision_part + jnp.einsum(
            "cki,ci->ck",
            inner,
            own_wide,
            precision=lax.Precision.HIGHEST,
            preferred_element_type=jnp.float32,
        )
    collision = lax.all_to_all(collision_part, "cell", split_axis=0, concat_axis=1, tiled=True)
    extended = with_halo(fields, (("cell", 1),), 2)
    wide = extended[0].astype(jnp.float32)
    prior_flag = shifted(face_limiter[:, -1:], "cell", 1)
    flags = jnp.concatenate([prior_flag, face_limiter], axis=1)[0][:, None]
    lower = wide[1:-1] - wide[:-2]
    upper = wide[2:] - wide[1:-1]
    slope_one = minmod_two(lower, upper)
    slope_two = minmod_three(2.0 * lower, 0.5 * (lower + upper), 2.0 * upper)
    zero = jnp.zeros((cells + 1, wide.shape[1]), jnp.float32)
    here = jnp.where(flags == 1, slope_one[:-1], jnp.where(flags == 2, slope_two[:-1], zero))
    there = jnp.where(flags == 1, slope_one[1:], jnp.where(flags == 2, slope_two[1:], zero))
    left_state = wide[1 : cells + 2] + 0.5 * here
    right_state = wide[2 : cells + 3] - 0.5 * there
    flux = jnp.dot(
        left_state,
        plus_flux[0],
        precision=lax.Precision.HIGHEST,
        preferred_element_type=jnp.float32,
    )
    flux = flux + jnp.dot(
        right_state,
        minus_flux[0],
        precision=lax.Precision.HIGHEST,
        preferred_element_type=jnp.float32,
    )
    center = wide[2 : cells + 2]
    new_field = center + 0.4 * (flux[:-1] - flux[1:]) + 0.5 * collision
    return (new_field[None], collision[None])


def solution(mesh):
    placed = (
        P("spec", "cell", None),
        P("spec", "cell", None, None),
        P(),
        P("spec", None, None),
        P("spec", None, None),
        P("spec", "cell"),
    )
    return jax.shard_map(
        local,
        mesh=mesh,
        in_specs=placed,
        out_specs=(P("spec", "cell", None), P("spec", "cell", None)),
        check_vma=False,
    )
```

profile of v0, /device:TPU:0, one launch (start us, length us, event | category | flops | bytes accessed | tf_op | source)
XLA Modules:
  0.0 144.8 jit_solution(16800425540163569697)
XLA Ops:
  7.2 7.1 %all_gather.6 = bf16[4,32,384]{2,1,0:T(8,128)(2,1)} all-gather(bf16[1,32,384]{2,1,0:T(8,128)(2,1)} %param.6), channel_id=1, replica_groups=mesh['cell'=32,'spec'=4] {'spec'}, dimensions={0}, use_global_device_ids=true | all-gather | bytes 122880 | tf_op jit(solution)/shard_map/all_gather | solution.py:44
  14.4 0.7 fusion.46
  15.1 8.6 %collective-permute-start.1 = (bf16[1,2,384]{2,1,0:T(2,128)(2,1)S(1)}, bf16[1,2,384]{2,1,0:T(2,128)(2,1)S(1)}, u32[]{:S(2)}, u32[]{:S(2)}) collective-permute-start(bf16[1,2,384]{2,1,0:T(2,128)(2,1)S(1)} %get-tuple-element.9), channel_id=1, source_target_pairs={{4,0},{8,4},{12,8},{16,12},{20,16},{24,20},{28,24},{32,28},{36,32}... | collective-permute-start | bytes 4616 | tf_op jit(solution)/shard_map/ppermute | solution.py:15
  23.6 1.3 slice.92
  24.9 0.7 constant_dynamic-slice_fusion
  25.6 0.6 fusion.47
  28.7 5.7 %collective-permute-done.2 = s32[1,1]{1,0:T(1,128)} collective-permute-done((s32[1,1]{1,0:T(1,128)}, s32[1,1]{1,0:T(1,128)}, u32[]{:S(2)}, u32[]{:S(2)}) %collective-permute-start.2) | collective-permute-done | bytes 36 | tf_op jit(solution)/shard_map/ppermute | solution.py:22
  34.4 1.4 compare_bitcast_fusion.1
  35.7 0.8 maximum_convert_fusion
  37.1 54.5 %all-gather.2.cloned.1.call-done = bf16[4,1024,384]{2,1,0:T(8,128)(2,1)} async-done(((bf16[4,32,384]{2,1,0:T(8,128)(2,1)}), bf16[4,1024,384]{2,1,0:T(8,128)(2,1)}) %all-gather.2.cloned.1.call-update) | async-done | bytes 3145744 | tf_op jit(solution)/shard_map/all_gather | solution.py:45
  91.5 1.2 bitcast_convert_fusion
  92.8 1.6 %copy.39 = f32[1024,384]{0,1:T(8,128)} copy(f32[1024,384]{1,0:T(8,128)S(1)} %bitcast_convert_fusion) | data formatting | bytes 3145728
  94.4 7.9 %fusion = f32[1024,12]{0,1:T(8,128)S(1)} fusion(f32[1024,384]{0,1:T(8,128)} %copy.39, bf16[4,12,384,384]{3,2,1,0:T(8,128)(2,1)} %param.7, s32[]{:T(128)S(6)} %select_n.49, bf16[4,1024,384]{2,1,0:T(8,128)(2,1)} %all-gather.2.cloned.1.call-done), kind=kOutput, calls=%fused_computation.1 | convolution fusion | flops 3633303552 | bytes 5947396 | tf_op jit(solution)/shard_map/cj,kij->cki/dot_general | solution.py:53
  102.6 5.6 %fusion.1 = f32[1024,12]{0,1:T(8,128)S(1)} fusion(f32[1024,384]{0,1:T(8,128)S(1)} %copy-done.1, bf16[4,12,384,384]{3,2,1,0:T(8,128)(2,1)S(1)} %copy-done.4, s32[]{:T(128)S(6)} %select_n.48, bf16[4,1024,384]{2,1,0:T(8,128)(2,1)S(1)} %copy-done.3), kind=kOutput, calls=%fused_computation.3 | convolution fusion | flops 3633303552 | bytes 5947396 | tf_op jit(solution)/shard_map/cj,kij->cki/dot_general | solution.py:53
  108.2 5.6 %fusion.3 = f32[1024,12]{0,1:T(8,128)S(1)} fusion(f32[1024,384]{0,1:T(8,128)S(1)} %copy-done.1, bf16[4,12,384,384]{3,2,1,0:T(8,128)(2,1)S(1)} %copy-done.4, s32[]{:T(128)S(6)} %select_n.46, bf16[4,1024,384]{2,1,0:T(8,128)(2,1)S(1)} %copy-done.3), kind=kOutput, calls=%fused_computation.7 | convolution fusion | flops 3633303552 | bytes 5947396 | tf_op jit(solution)/shard_map/cj,kij->cki/dot_general | solution.py:53
  113.9 5.6 %fusion.2 = f32[1024,12]{0,1:T(8,128)S(1)} fusion(f32[1024,384]{0,1:T(8,128)S(1)} %copy-done.1, bf16[4,12,384,384]{3,2,1,0:T(8,128)(2,1)S(1)} %copy-done.4, s32[]{:T(128)S(6)} %select_n.47, bf16[4,1024,384]{2,1,0:T(8,128)(2,1)S(1)} %copy-done.3), kind=kOutput, calls=%fused_computation.5 | convolution fusion | flops 3633303552 | bytes 5947396 | tf_op jit(solution)/shard_map/cj,kij->cki/dot_general | solution.py:53
  119.8 0.8 reshape.94
  120.5 4.7 %all-to-all-start = ((f32[32,1,384]{2,1,0:T(1,128)}), f32[32,1,384]{2,1,0:T(1,128)S(1)}, u32[]{:S(2)}, u32[]{:S(2)}) async-start(f32[32,1,384]{2,1,0:T(1,128)} %reshape.94), calls=%async_computation | async-start | bytes 98304 | tf_op jit(solution)/shard_map/all_to_all | solution.py:61
  125.2 0.5 convolution_add_fusion
  125.7 9.3 %all-to-all-done = f32[32,1,384]{2,1,0:T(1,128)S(1)} async-done(((f32[32,1,384]{2,1,0:T(1,128)}), f32[32,1,384]{2,1,0:T(1,128)S(1)}, u32[]{:S(2)}, u32[]{:S(2)}) %all-to-all-start) | async-done | bytes 49184 | tf_op jit(solution)/shard_map/all_to_all | solution.py:61
  135.0 0.5 broadcast.69
  135.5 0.8 reduce.8
  136.6 0.7 copy.14
  137.3 0.6 fusion.29
  (27 shorter events, 1.5 us)
Async XLA Ops:
  7.2 29.4 %copy-start = (f32[1,384,384]{2,1,0:T(8,128)S(1)}, f32[1,384,384]{2,1,0:T(8,128)}, u32[]{:S(2)}) copy-start(f32[1,384,384]{2,1,0:T(8,128)} %param.9) | copy-start | bytes 1769476
  7.2 84.3 %all-gather.2.cloned.1.call-start = ((), (), s32[]{:S(2)}) async-start(), calls=%async_computation.1 | async-start | bytes 3244032 | tf_op jit(solution)/shard_map/all_gather | solution.py:45
  15.1 20.7 %collective-permute-start.1 = (bf16[1,2,384]{2,1,0:T(2,128)(2,1)S(1)}, bf16[1,2,384]{2,1,0:T(2,128)(2,1)S(1)}, u32[]{:S(2)}, u32[]{:S(2)}) collective-permute-start(bf16[1,2,384]{2,1,0:T(2,128)(2,1)S(1)} %get-tuple-element.9), channel_id=1, source_target_pairs={{4,0},{8,4},{12,8},{16,12},{20,16},{24,20},{28,24},{32,28},{36,32}... | collective-permute-start | bytes 4616 | tf_op jit(solution)/shard_map/ppermute | solution.py:15
  23.6 12.1 %collective-permute-start = (bf16[1,2,384]{2,1,0:T(2,128)(2,1)S(1)}, bf16[1,2,384]{2,1,0:T(2,128)(2,1)S(1)}, u32[]{:S(2)}, u32[]{:S(2)}) collective-permute-start(bf16[1,2,384]{2,1,0:T(2,128)(2,1)S(1)} %get-tuple-element.8), channel_id=1, source_target_pairs={{0,4},{4,8},{8,12},{12,16},{16,20},{20,24},{24,28},{28,32},{32,36}... | collective-permute-start | bytes 4616 | tf_op jit(solution)/shard_map/ppermute | solution.py:14
  24.9 9.5 %collective-permute-start.2 = (s32[1,1]{1,0:T(1,128)}, s32[1,1]{1,0:T(1,128)}, u32[]{:S(2)}, u32[]{:S(2)}) collective-permute-start(s32[1,1]{1,0:T(1,128)} %slice.92), channel_id=1, source_target_pairs={{0,4},{4,8},{8,12},{12,16},{16,20},{20,24},{24,28},{28,32},{32,36}... | collective-permute-start | bytes 20 | tf_op jit(solution)/shard_map/ppermute | solution.py:22
  94.4 7.9 %copy-start.1 = (f32[1024,384]{0,1:T(8,128)S(1)}, f32[1024,384]{0,1:T(8,128)}, u32[]{:S(2)}) copy-start(f32[1024,384]{0,1:T(8,128)} %copy.39) | copy-start | bytes 4718596
  94.4 7.9 %copy-start.3 = (bf16[4,1024,384]{2,1,0:T(8,128)(2,1)S(1)}, bf16[4,1024,384]{2,1,0:T(8,128)(2,1)}, u32[]{:S(2)}) copy-start(bf16[4,1024,384]{2,1,0:T(8,128)(2,1)} %all-gather.2.cloned.1.call-done) | copy-start | bytes 9437188
  94.4 8.2 %copy-start.4 = (bf16[4,12,384,384]{3,2,1,0:T(8,128)(2,1)S(1)}, bf16[4,12,384,384]{3,2,1,0:T(8,128)(2,1)}, u32[]{:S(2)}) copy-start(bf16[4,12,384,384]{3,2,1,0:T(8,128)(2,1)} %param.7) | copy-start | bytes 42467332
  113.8 11.4 %copy-start.2 = (f32[1,384,384]{2,1,0:T(8,128)S(1)}, f32[1,384,384]{2,1,0:T(8,128)}, u32[]{:S(2)}) copy-start(f32[1,384,384]{2,1,0:T(8,128)} %param.10) | copy-start | bytes 1769476
  120.5 14.5 %all-to-all-start = ((f32[32,1,384]{2,1,0:T(1,128)}), f32[32,1,384]{2,1,0:T(1,128)S(1)}, u32[]{:S(2)}, u32[]{:S(2)}) async-start(f32[32,1,384]{2,1,0:T(1,128)} %reshape.94), calls=%async_computation | async-start | bytes 98304 | tf_op jit(solution)/shard_map/all_to_all | solution.py:61
Sparse Core Ops, SparseCore 0:
  14.5 76.9 all-gather.1
where the time goes:
time: 145 us
  waiting for transfers between devices  69.4 us (48%)
  matrix products  25.7 us (18%)
  between operations  16.7 us (12%)
  starting transfers between devices  13.3 us (9%)
  local copies, waits for them, and re-layouts  7.71 us (5%)
  blocking collectives  7.11 us (5%)
  other arithmetic  4.88 us (3%)
    all_gather x1, waiting for transfers between devices, local(): gathered = lax.all_gather(all_species, 'cell', axis=1, tiled=True)  54.5 us
    dot_general x4, matrix products, local(): jnp.einsum('cj,kij->cki', partner_rows, tensor, preferred_element_type=jn...  24.7 us
    all_to_all x1, waiting for transfers between devices, local(): lax.all_to_all(collision_part, 'cell', split_axis=0, concat_axis=1, tiled...  9.3 us
    ppermute x1, starting transfers between devices, with_halo(): after = lax.ppermute(leading, axis, down)  8.57 us
    all_gather x1, blocking collectives, local(): all_species = lax.all_gather(fields, 'spec', axis=0, tiled=True)  7.11 us
    ppermute x1, waiting for transfers between devices, shifted(): return lax.ppermute(x, axis, [(i, (i + by) % size) for i in range(size)])  5.67 us
    all_to_all x1, starting transfers between devices, local(): lax.all_to_all(collision_part, 'cell', split_axis=0, concat_axis=1, tiled...  4.7 us
    unnamed x14, local copies, waits for them, and re-layouts  3.55 us
  transfers between devices with their start and end apart: 5, of which 3 were waited for; matrix products, arithmetic and copies ran while one was open for 4% of the time, Pallas kernels for 0%

commit v1 on v0

--- a/solution.py
+++ b/solution.py
@@ -42,7 +42,9 @@
     out_modes = tensors.shape[1]
     table_row = lax.dynamic_index_in_dim(pair_table, owner, 0, keepdims=False)
     all_species = lax.all_gather(fields, "spec", axis=0, tiled=True)
-    gathered = lax.all_gather(all_species, "cell", axis=1, tiled=True)
+    gathered = jnp.concatenate(
+        lax.all_to_all(jnp.stack([all_species] * lax.axis_size("cell")), "cell", 0, 0), axis=1
+    )
     own_rows = lax.dynamic_index_in_dim(gathered, owner, 0, keepdims=True)
     own_wide = own_rows[0].astype(jnp.float32)
     collision_part = jnp.zeros((total_cells, out_modes), jnp.float32)

time: 145 us -> 119 us (0.82)
  waiting for transfers between devices: 69.4 us -> 36.6 us
  starting transfers between devices: 13.3 us -> 26.6 us
  between operations: 16.7 us -> 3.48 us
  local copies, waits for them, and re-layouts: 7.71 us -> 15.9 us
    all_gather x1 -> x0, waiting for transfers between devices: 54.5 us -> none  [local(): gathered = lax.all_gather(all_species, 'cell', axis=1, tiled=True)]
    ppermute x1, waiting for transfers between devices: 5.67 us -> 27.3 us  [shifted(): return lax.ppermute(x, axis, [(i, (i + by) % size) for i in range(size)])]
    all_to_all x0 -> x1, starting transfers between devices: none -> 11 us  [local(): lax.all_to_all(jnp.stack([all_species] * lax.axis_size('cell')), 'cell',...]
    all_to_all x1, starting transfers between devices: 4.7 us -> 7.95 us  [local(): lax.all_to_all(collision_part, 'cell', split_axis=0, concat_axis=1, tiled...]
    slice x0 -> x1, local copies, waits for them, and re-layouts: none -> 2.33 us  [local(): partner_rows = gathered[partner]]
    all_to_all x0 -> x1, local copies, waits for them, and re-layouts: none -> 2.29 us  [local(): lax.all_to_all(jnp.stack([all_species] * lax.axis_size('cell')), 'cell',...]
    another operation x0 -> x1, local copies, waits for them, and re-layouts: none -> 2.17 us  [local(): jnp.stack([all_species] * lax.axis_size('cell'))]
    unnamed x14 -> x20, local copies, waits for them, and re-layouts: 3.55 us -> 4.89 us
  transfers between devices with their start and end apart: 5 -> 5, of which waited for: 3 -> 2; matrix products, arithmetic and copies ran while one was open for 4% -> 5% of each run, Pallas kernels for 0% -> 0%
where the time goes in v1:
time: 119 us; the launch traced here: 118 us
  waiting for transfers between devices  36.6 us (31%)
  starting transfers between devices  26.6 us (22%)
  matrix products  25.7 us (22%)
  local copies, waits for them, and re-layouts  15.9 us (13%)
  blocking collectives  5.67 us (5%)
  other arithmetic  3.75 us (3%)
  between operations  3.48 us (3%)
    ppermute x1, waiting for transfers between devices, shifted(): return lax.ppermute(x, axis, [(i, (i + by) % size) for i in range(size)])  27.3 us
    dot_general x4, matrix products, local(): jnp.einsum('cj,kij->cki', partner_rows, tensor, preferred_element_type=jn...  24.8 us
    all_to_all x1, starting transfers between devices, local(): lax.all_to_all(jnp.stack([all_species] * lax.axis_size('cell')), 'cell',...  11 us
    all_to_all x1, waiting for transfers between devices, local(): lax.all_to_all(collision_part, 'cell', split_axis=0, concat_axis=1, tiled...  9.3 us
    all_to_all x1, starting transfers between devices, local(): lax.all_to_all(collision_part, 'cell', split_axis=0, concat_axis=1, tiled...  7.95 us
    ppermute x1, starting transfers between devices, with_halo(): after = lax.ppermute(leading, axis, down)  7.54 us
    all_gather x1, blocking collectives, local(): all_species = lax.all_gather(fields, 'spec', axis=0, tiled=True)  5.67 us
    unnamed x20, local copies, waits for them, and re-layouts  4.89 us
  transfers between devices with their start and end apart: 5, of which 2 were waited for; matrix products, arithmetic and copies ran while one was open for 5% of the time, Pallas kernels for 0%

profile of v1, /device:TPU:0, one launch (start us, length us, event | category | flops | bytes accessed | tf_op | source)
XLA Modules:
  0.0 117.8 jit_solution(5173710136335667267)
XLA Ops:
  0.6 5.7 %all_gather.3 = bf16[4,32,384]{2,1,0:T(8,128)(2,1)S(1)} all-gather(bf16[1,32,384]{2,1,0:T(8,128)(2,1)} %param.6), channel_id=1, replica_groups=mesh['cell'=32,'spec'=4] {'spec'}, dimensions={0}, use_global_device_ids=true | all-gather | bytes 122880 | tf_op jit(solution)/shard_map/all_gather | solution.py:44
  6.3 2.2 %stack.2 = bf16[32,4,32,384]{3,2,1,0:T(8,128)(2,1)} broadcast(bf16[4,32,384]{2,1,0:T(8,128)(2,1)S(1)} %all_gather.3), dimensions={1,2,3} | broadcast | bytes 3244032 | tf_op jit(solution)/shard_map/stack | solution.py:46
  8.5 11.0 %all-to-all-start = ((bf16[32,4,32,384]{3,2,1,0:T(8,128)(2,1)}), bf16[32,4,32,384]{3,2,1,0:T(8,128)(2,1)}, u32[]{:S(2)}, u32[]{:S(2)}) async-start(bf16[32,4,32,384]{3,2,1,0:T(8,128)(2,1)} %stack.2), calls=%async_computation | async-start | bytes 6291456 | tf_op jit(solution)/shard_map/all_to_all | solution.py:46
  19.5 0.7 fusion.47
  20.2 7.5 %collective-permute-start.1 = (bf16[1,2,384]{2,1,0:T(2,128)(2,1)S(1)}, bf16[1,2,384]{2,1,0:T(2,128)(2,1)S(1)}, u32[]{:S(2)}, u32[]{:S(2)}) collective-permute-start(bf16[1,2,384]{2,1,0:T(2,128)(2,1)S(1)} %get-tuple-element.15), channel_id=1, source_target_pairs={{4,0},{8,4},{12,8},{16,12},{20,16},{24,20},{28,24},{32,28},{36,32}... | collective-permute-start | bytes 4616 | tf_op jit(solution)/shard_map/ppermute | solution.py:15
  27.8 1.3 %slice.96 = s32[1,1]{1,0:T(1,128)} slice(s32[1,32]{1,0:T(1,128)} %param.11), slice={[0:1], [31:32]} | slice | bytes 8 | tf_op jit(solution)/shard_map/slice | solution.py:66
  29.1 0.7 constant_dynamic-slice_fusion
  29.8 0.7 fusion.48
  33.1 27.3 %collective-permute-done.2 = s32[1,1]{1,0:T(1,128)} collective-permute-done((s32[1,1]{1,0:T(1,128)}, s32[1,1]{1,0:T(1,128)}, u32[]{:S(2)}, u32[]{:S(2)}) %collective-permute-start.2) | collective-permute-done | bytes 36 | tf_op jit(solution)/shard_map/ppermute | solution.py:22
  60.4 1.4 %compare_bitcast_fusion.1 = (pred[33]{0:T(512)(128)(4,1)S(1)}, pred[33]{0:T(512)(128)(4,1)S(1)}) fusion(s32[1,32]{1,0:T(1,128)} %param.11, s32[1,1]{1,0:T(1,128)} %collective-permute-done.2), kind=kLoop, calls=%fused_computation.62 | loop fusion | flops 99 | bytes 198 | tf_op jit(solution)/shard_map/eq | solution.py:73
  61.8 0.8 maximum_convert_fusion
  63.1 2.3 %copy.45 = bf16[32,4,32,384]{3,2,0,1:T(8,128)(2,1)S(1)} copy(bf16[32,4,32,384]{3,2,1,0:T(8,128)(2,1)} %all-to-all-done) | data formatting | bytes 6291456 | tf_op jit(solution)/shard_map/all_to_all | solution.py:46
  65.4 1.6 %copy-done.1 = bf16[32,4,32,384]{3,2,0,1:T(8,128)(2,1)} copy-done((bf16[32,4,32,384]{3,2,0,1:T(8,128)(2,1)}, bf16[32,4,32,384]{3,2,0,1:T(8,128)(2,1)S(1)}, u32[]{:S(2)}) %copy-start.1) | copy-done | bytes 3145752
  67.2 1.6 %copy.40 = f32[1024,384]{0,1:T(8,128)} copy(f32[1024,384]{1,0:T(8,128)S(1)} %bitcast_convert_fusion) | data formatting | bytes 3145728
  68.8 2.3 %fusion.46 = (bf16[1,32,32,384]{3,2,1,0:T(8,128)(2,1)S(1)}, bf16[1,32,32,384]{3,2,1,0:T(8,128)(2,1)S(1)}, bf16[1,32,32,384]{3,2,1,0:T(8,128)(2,1)S(1)}, bf16[1,32,32,384]{3,2,1,0:T(8,128)(2,1)S(1)}) fusion(bf16[4,32,32,384]{3,2,1,0:T(8,128)(2,1)} %bitcast.137), kind=kLoop, calls=%fused_computation.74 | loop fusion | bytes 6291456 | tf_op jit(solution)/shard_map/slice | solution.py:52
  71.2 7.9 %fusion = f32[1024,12]{0,1:T(8,128)S(1)} fusion(f32[1024,384]{0,1:T(8,128)} %copy.40, bf16[1024,384,1]{1,0,2:T(8,128)(2,1)S(1)} %bitcast.142, bf16[4,12,384,384]{3,2,1,0:T(8,128)(2,1)} %param.7, s32[]{:T(128)S(6)} %select_n.49), kind=kOutput, calls=%fused_computation.1 | convolution fusion | flops 3633303552 | bytes 5947396 | tf_op jit(solution)/shard_map/cj,kij->cki/dot_general | solution.py:55
  79.2 5.6 %fusion.1 = f32[1024,12]{0,1:T(8,128)S(1)} fusion(f32[1024,384]{0,1:T(8,128)S(1)} %copy-done.2, bf16[1024,384,1]{1,0,2:T(8,128)(2,1)S(1)} %bitcast.141, bf16[4,12,384,384]{3,2,1,0:T(8,128)(2,1)S(1)} %bitcast.144, s32[]{:T(128)S(6)} %select_n.48), kind=kOutput, calls=%fused_computation.3 | convolution fusion | flops 3633303552 | bytes 5947396 | tf_op jit(solution)/shard_map/cj,kij->cki/dot_general | solution.py:55
  84.8 5.6 %fusion.3 = f32[1024,12]{0,1:T(8,128)S(1)} fusion(f32[1024,384]{0,1:T(8,128)S(1)} %copy-done.2, bf16[1024,384,1]{1,0,2:T(8,128)(2,1)S(1)} %bitcast.140, bf16[4,12,384,384]{3,2,1,0:T(8,128)(2,1)S(1)} %bitcast.144, s32[]{:T(128)S(6)} %select_n.46), kind=kOutput, calls=%fused_computation.7 | convolution fusion | flops 3633303552 | bytes 5947396 | tf_op jit(solution)/shard_map/cj,kij->cki/dot_general | solution.py:55
  90.4 5.6 %fusion.2 = f32[1024,12]{0,1:T(8,128)S(1)} fusion(f32[1024,384]{0,1:T(8,128)S(1)} %copy-done.2, bf16[1024,384,1]{1,0,2:T(8,128)(2,1)S(1)} %bitcast.139, bf16[4,12,384,384]{3,2,1,0:T(8,128)(2,1)S(1)} %bitcast.144, s32[]{:T(128)S(6)} %select_n.47), kind=kOutput, calls=%fused_computation.5 | convolution fusion | flops 3633303552 | bytes 5947396 | tf_op jit(solution)/shard_map/cj,kij->cki/dot_general | solution.py:55
  96.3 0.8 reshape.112
  97.1 7.9 %all-to-all-start.1 = ((f32[32,1,384]{2,1,0:T(1,128)}), f32[32,1,384]{2,1,0:T(1,128)S(1)}, u32[]{:S(2)}, u32[]{:S(2)}) async-start(f32[32,1,384]{2,1,0:T(1,128)} %reshape.112), calls=%async_computation.1 | async-start | bytes 98304 | tf_op jit(solution)/shard_map/all_to_all | solution.py:63
  105.5 9.3 %all-to-all-done.1 = f32[32,1,384]{2,1,0:T(1,128)S(1)} async-done(((f32[32,1,384]{2,1,0:T(1,128)}), f32[32,1,384]{2,1,0:T(1,128)S(1)}, u32[]{:S(2)}, u32[]{:S(2)}) %all-to-all-start.1) | async-done | bytes 49184 | tf_op jit(solution)/shard_map/all_to_all | solution.py:63
  115.3 0.8 reduce.8
  116.4 0.7 copy.15
  (36 shorter events, 3.0 us)
Async XLA Ops:
  0.6 62.0 %copy-start = (f32[1,384,384]{2,1,0:T(8,128)S(1)}, f32[1,384,384]{2,1,0:T(8,128)}, u32[]{:S(2)}) copy-start(f32[1,384,384]{2,1,0:T(8,128)} %param.9) | copy-start | bytes 1769476
  8.5 54.6 %all-to-all-start = ((bf16[32,4,32,384]{3,2,1,0:T(8,128)(2,1)}), bf16[32,4,32,384]{3,2,1,0:T(8,128)(2,1)}, u32[]{:S(2)}, u32[]{:S(2)}) async-start(bf16[32,4,32,384]{3,2,1,0:T(8,128)(2,1)} %stack.2), calls=%async_computation | async-start | bytes 6291456 | tf_op jit(solution)/shard_map/all_to_all | solution.py:46
  20.2 41.6 %collective-permute-start.1 = (bf16[1,2,384]{2,1,0:T(2,128)(2,1)S(1)}, bf16[1,2,384]{2,1,0:T(2,128)(2,1)S(1)}, u32[]{:S(2)}, u32[]{:S(2)}) collective-permute-start(bf16[1,2,384]{2,1,0:T(2,128)(2,1)S(1)} %get-tuple-element.15), channel_id=1, source_target_pairs={{4,0},{8,4},{12,8},{16,12},{20,16},{24,20},{28,24},{32,28},{36,32}... | collective-permute-start | bytes 4616 | tf_op jit(solution)/shard_map/ppermute | solution.py:15
  27.8 34.0 %collective-permute-start = (bf16[1,2,384]{2,1,0:T(2,128)(2,1)S(1)}, bf16[1,2,384]{2,1,0:T(2,128)(2,1)S(1)}, u32[]{:S(2)}, u32[]{:S(2)}) collective-permute-start(bf16[1,2,384]{2,1,0:T(2,128)(2,1)S(1)} %get-tuple-element.14), channel_id=1, source_target_pairs={{0,4},{4,8},{8,12},{12,16},{16,20},{20,24},{24,28},{28,32},{32,36}... | collective-permute-start | bytes 4616 | tf_op jit(solution)/shard_map/ppermute | solution.py:14
  29.0 31.4 %collective-permute-start.2 = (s32[1,1]{1,0:T(1,128)}, s32[1,1]{1,0:T(1,128)}, u32[]{:S(2)}, u32[]{:S(2)}) collective-permute-start(s32[1,1]{1,0:T(1,128)} %slice.96), channel_id=1, source_target_pairs={{0,4},{4,8},{8,12},{12,16},{16,20},{20,24},{24,28},{28,32},{32,36}... | collective-permute-start | bytes 20 | tf_op jit(solution)/shard_map/ppermute | solution.py:22
  65.4 1.6 %copy-start.1 = (bf16[32,4,32,384]{3,2,0,1:T(8,128)(2,1)}, bf16[32,4,32,384]{3,2,0,1:T(8,128)(2,1)S(1)}, u32[]{:S(2)}) copy-start(bf16[32,4,32,384]{3,2,0,1:T(8,128)(2,1)S(1)} %copy.45) | copy-start | bytes 9437188
  68.8 10.3 %copy-start.2 = (f32[1024,384]{0,1:T(8,128)S(1)}, f32[1024,384]{0,1:T(8,128)}, u32[]{:S(2)}) copy-start(f32[1024,384]{0,1:T(8,128)} %copy.40) | copy-start | bytes 4718596
  68.8 10.3 %slice-start = ((s8[14155776]{0:T(1024)(128)(4,1)}), s8[4194304]{0:T(1024)(128)(4,1)S(1)}, s32[]{:S(2)}) async-start(s8[14155776]{0:T(1024)(128)(4,1)} %bitcast.143), calls=%async_computation.2 | async-start | bytes 8388608
  71.1 8.0 %slice-start.1 = ((s8[14155776]{0:T(1024)(128)(4,1)}), s8[4194304]{0:T(1024)(128)(4,1)S(1)}, s32[]{:S(2)}) async-start(s8[14155776]{0:T(1024)(128)(4,1)} %bitcast.143), calls=%async_computation.3 | async-start | bytes 8388608
  71.1 8.0 %slice-start.2 = ((s8[14155776]{0:T(1024)(128)(4,1)}), s8[4194304]{0:T(1024)(128)(4,1)S(1)}, s32[]{:S(2)}) async-start(s8[14155776]{0:T(1024)(128)(4,1)} %bitcast.143), calls=%async_computation.4 | async-start | bytes 8388608
  71.2 8.0 %slice-start.3 = ((s8[14155776]{0:T(1024)(128)(4,1)}), s8[1572864]{0:T(1024)(128)(4,1)S(1)}, s32[]{:S(2)}) async-start(s8[14155776]{0:T(1024)(128)(4,1)} %bitcast.143), calls=%async_computation.5 | async-start | bytes 3145728
  90.4 14.6 %copy-start.3 = (f32[1,384,384]{2,1,0:T(8,128)S(1)}, f32[1,384,384]{2,1,0:T(8,128)}, u32[]{:S(2)}) copy-start(f32[1,384,384]{2,1,0:T(8,128)} %param.10) | copy-start | bytes 1769476
  97.1 17.7 %all-to-all-start.1 = ((f32[32,1,384]{2,1,0:T(1,128)}), f32[32,1,384]{2,1,0:T(1,128)S(1)}, u32[]{:S(2)}, u32[]{:S(2)}) async-start(f32[32,1,384]{2,1,0:T(1,128)} %reshape.112), calls=%async_computation.1 | async-start | bytes 98304 | tf_op jit(solution)/shard_map/all_to_all | solution.py:63
